TPU v7x, 768 devices: a whole 4x8x12 slice. The times are simulated.
768 devices in a mesh: dom: 192 (over y, z, core), depth: 4 (over x).
Axes of the slice: x: 4, y: 8, z: 12, core: 2. Of those that a mesh axis runs over, the one named last changes fastest.
Arguments:
- adjoint_now: float32 [3, 768, 68, 128], P(None, 'dom', 'depth'), may hold values from -6 to 6
- adjoint_next: float32 [3, 768, 68, 128], P(None, 'dom', 'depth'), may hold values from -6 to 6
- lame_first: float32 [192, 16, 32], P('dom', 'depth'), may hold values from 1 to 3
- shear_modulus: float32 [192, 16, 32], P('dom', 'depth'), may hold values from 1 to 3
- density: float32 [768, 68, 128], P('dom', 'depth'), may hold values from 1 to 3
- branch_flags: int32 [4, 4, 768, 128], P(None, 'depth', 'dom'), may hold values from 0 to 2
- weak_slope: float32 [4, 768, 128], P('depth', 'dom'), may hold values from 0.1 to 0.5
- normal_stress: float32 [4, 768, 128], P('depth', 'dom'), may hold values from 1 to 10
- patch_owner: int32 [4, 768], P('depth', 'dom'), may hold values from 0 to 383, as said below
Outputs:
- earlier_state: float32 [3, 768, 68, 128], P(None, 'dom', 'depth')
- later_state: float32 [3, 768, 68, 128], P(None, 'dom', 'depth')
- patch_gradient: float32 [4, 384, 128], P('depth', 'dom')
Inputs may be any that keep to these rules, and one draw needn't show every extreme that they name: `patch_owner`: patch p is owned by dom index p // 2; a column held by dom index d belongs to a patch whose owner is at most 2 indices of dom from d.
All inputs are finite; a program needn't handle non-finite values.
Results may differ from a plain program's by a relative error of at most 0.0001.
Values sent between devices are 32-bit elements; how exact they have to be, the bound alone decides.
A program may use at most 32 MiB of HBM per device.

v0:
```python
import functools
import math

import jax
import jax.numpy as jnp
import numpy as np
from jax import lax
from jax.experimental import pallas as pl
from jax.experimental.pallas import tpu as pltpu
from jax.sharding import PartitionSpec as P


MESH = pl.DeviceIdType.MESH
STEPS = 4
ROWS = 80
DT2 = 0.01 * 0.01
LOCK = 0.5
W5 = [0.1, 49.0 / 90.0, 32.0 / 45.0, 49.0 / 90.0, 0.1]
OFFSETS = (-2, -1, 1, 2)
f32 = jnp.float32


def slopes5():
    pts = [-1.0, -math.sqrt(3.0 / 7.0), 0.0, math.sqrt(3.0 / 7.0), 1.0]
    prod = [np.prod([pts[a] - pts[b] for b in range(5) if b != a]) for a in range(5)]
    d = np.zeros((5, 5))
    for a in range(5):
        for b in range(5):
            if a == b:
                d[a, b] = sum(1.0 / (pts[a] - pts[o]) for o in range(5) if o != a)
            else:
                d[a, b] = prod[a] / prod[b] / (pts[a] - pts[b])
    d[2, 2] = 0.0
    return 2.0 * d


D5 = slopes5()


def apply5(m, v):
    e0, e1, o0, o1 = v[0] + v[4], v[1] + v[3], v[0] - v[4], v[1] - v[3]
    out = [None] * 5
    for q in (0, 1):
        a = (
            float((m[q, 0] + m[q, 4]) / 2) * e0
            + float((m[q, 1] + m[q, 3]) / 2) * e1
            + float(m[q, 2]) * v[2]
        )
        b = float((m[q, 0] - m[q, 4]) / 2) * o0 + float((m[q, 1] - m[q, 3]) / 2) * o1
        out[q] = b + a
        out[4 - q] = b - a
    out[2] = float((m[2, 0] - m[2, 4]) / 2) * o0 + float((m[2, 1] - m[2, 3]) / 2) * o1
    return out


def wkey(a, b):
    a, b = min(a, 4 - a), min(b, 4 - b)
    a, b = min(a, b), max(a, b)
    return {(0, 0): 0, (0, 1): 1, (0, 2): 2, (1, 1): 3, (1, 2): 4, (2, 2): 5}[(a, b)]


WPAIR = [(0, 0), (0, 1), (0, 2), (1, 1), (1, 2), (2, 2)]


def rblk(c, yl, zl):
    return (c * 5 + yl) * 5 + zl


def kernel(
    nd,
    ndp,
    now,
    nxt,
    lam,
    mu,
    dens,
    flags,
    slope,
    ns,
    owner,
    out_cur,
    out_fol,
    out_patch,
    nowv,
    nxtv,
    densv,
    lamv,
    muv,
    flagv,
    slopev,
    nsv,
    ownv,
    gnow,
    gnxt,
    gdens,
    gflag,
    gslope,
    stage,
    S,
    F,
    GY,
    FX,
    FY,
    IM,
    IMP,
    CONST,
    TH,
    grad,
    send_dom,
    recv_dom,
    send_dep,
    recv_dep,
    psend,
    precv,
    outv,
    patchv,
    lsem,
    isend,
    irecv,
    dsend,
    drecv,
    fsend,
    frecv,
    pss,
    prs,
    osem,
):
    me = lax.axis_index("dom")
    my = lax.axis_index("depth")
    up = lax.rem(my + 1, ndp)
    dn = lax.rem(my + ndp - 1, ndp)
    has_l = me > 0
    has_r = me < nd - 1

    locals_ = [
        pltpu.make_async_copy(a, b, lsem.at[i])
        for i, (a, b) in enumerate(
            [
                (now, nowv),
                (nxt, nxtv),
                (dens, densv),
                (lam, lamv),
                (mu, muv),
                (flags, flagv),
                (slope, slopev),
                (ns, nsv),
                (owner, ownv),
            ]
        )
    ]
    for cp in locals_:
        cp.start()

    barrier = pltpu.get_barrier_semaphore()
    count = 2
    pl.semaphore_signal(barrier, inc=1, device_id=(me, up), device_id_type=MESH)
    pl.semaphore_signal(barrier, inc=1, device_id=(me, dn), device_id_type=MESH)
    for off, row in ((-1, my), (1, my), (-2, my), (2, my), (-1, up), (1, dn)):
        ok = jnp.logical_and(me + off >= 0, me + off < nd)
        count = count + ok.astype(jnp.int32)

        @pl.when(ok)
        def _(off=off, row=row):
            pl.semaphore_signal(
                barrier, inc=1, device_id=(me + off, row), device_id_type=MESH
            )

    pl.semaphore_wait(barrier, count)

    def remote(i, src, dst, to):
        return pltpu.make_async_remote_copy(
            src_ref=src,
            dst_ref=dst,
            send_sem=isend.at[i],
            recv_sem=irecv.at[i],
            device_id=to,
            device_id_type=MESH,
        )

    to_left = [
        remote(0, now.at[:, 0], gnow, (me - 1, my)),
        remote(1, nxt.at[:, 0], gnxt, (me - 1, my)),
        remote(2, dens.at[0], gdens, (me - 1, my)),
        remote(3, flags, gflag.at[0], (me - 1, my)),
        remote(4, slope, gslope.at[0], (me - 1, my)),
        remote(5, flags, gflag.at[1], (me - 1, up)),
        remote(6, slope, gslope.at[1], (me - 1, up)),
    ]
    to_up = [
        remote(7, flags, gflag.at[2], (me, up)),
        remote(8, slope, gslope.at[2], (me, up)),
    ]

    @pl.when(has_l)
    def _():
        for cp in to_left:
            cp.start()

    for cp in to_up:
        cp.start()

    lane = lax.broadcasted_iota(jnp.int32, (8, 128), 1)
    sub = lax.broadcasted_iota(jnp.int32, (8, 128), 0)
    blk = lane // 32
    ez = lane % 32
    to_packed = 4 * ez + blk
    to_natural = (lane % 4) * 32 + lane // 4
    b0, b1, b2, b3 = blk == 0, blk == 1, blk == 2, blk == 3

    def permute(x, idx):
        return jnp.take_along_axis(x, idx, axis=1)

    def roll(x, shift):
        shift = shift % 128
        return x if shift == 0 else pltpu.roll(x, shift, 1)

    def by_sub(vals):
        v = jnp.full((8, 128), 0.0, f32)
        for i, x in enumerate(vals):
            if x != 0.0:
                v = jnp.where(sub == i, float(x), v)
        return v

    for k in range(5):
        CONST[k] = by_sub(D5[:, k])
        CONST[5 + k] = by_sub(D5[k, :])

    stage[...] = jnp.zeros(stage.shape, f32)
    for i in range(75, ROWS):
        F[pl.ds(8 * i, 8), :] = jnp.zeros((8, 128), f32)
        S[0, pl.ds(8 * i, 8), :] = jnp.zeros((8, 128), f32)
        S[1, pl.ds(8 * i, 8), :] = jnp.zeros((8, 128), f32)

    def pick(r0, r1, r2, r3):
        return jnp.where(b0, r0, jnp.where(b1, r1, jnp.where(b2, r2, r3)))

    def to_elements(c, put, bottom):
        packed = [
            permute(stage[pl.ds(c * 192 + y, 8, stride=24), :], to_packed)
            for y in range(17)
        ]
        rolled = [[roll(v, 32 * s) for s in range(4)] for v in packed]
        for yl in range(5):
            for zl in range(4):
                v = pick(*[rolled[4 * e + yl][(e - zl) % 4] for e in range(4)])
                put(yl, zl, v)
                if zl == 0:
                    first = v
            put(yl, 4, jnp.where(ez == 31, bottom, roll(first, -1)))

    for cp in locals_:
        cp.wait()

    @pl.when(has_r)
    def _():
        for cp in to_left:
            cp.wait_recv()

    for cp in to_up:
        cp.wait_recv()

    def fill(own, ghost, slot):
        for c in range(3):
            for x in range(4):
                stage[pl.ds((c * 8 + x) * 24, 17), :] = own[c, x]
            stage[pl.ds((c * 8 + 4) * 24, 17), :] = jnp.where(has_r, ghost[c], 0.0)
        for c in range(3):

            def put(yl, zl, v, c=c):
                S[slot, pl.ds(8 * rblk(c, yl, zl), 8), :] = v

            to_elements(c, put, 0.0)

    fill(nowv, gnow, 0)
    fill(nxtv, gnxt, 1)

    for x in range(4):
        stage[pl.ds(x * 24, 17), :] = densv[x]
    stage[pl.ds(4 * 24, 17), :] = jnp.where(has_r, gdens[...], 1.0)
    wx = by_sub([0.2, W5[1], W5[2], W5[3], 0.2])
    wx = jnp.where(sub == 0, jnp.where(has_l, 0.2, 0.1), wx)
    live_x = jnp.logical_or(sub < 4, jnp.logical_and(sub == 4, has_r))

    def put_mass(yl, zl, v):
        if yl in (1, 2, 3):
            wy = W5[yl]
        else:
            wy = jnp.where(b0 if yl == 0 else b3, 0.1, 0.2)
        if zl in (1, 2, 3):
            wz = W5[zl]
        elif zl == 0:
            wz = jnp.where(ez == 0, 0.1, 0.2)
        else:
            wz = 0.2
        mass = v * wx * wy * wz
        live = jnp.logical_and(live_x, ez < 31) if zl == 4 else live_x
        IM[pl.ds(8 * (yl * 5 + zl), 8), :] = jnp.where(
            live, (8.0 * DT2) / jnp.where(live, mass, 1.0), 0.0
        )

    to_elements(0, put_mass, 1.0)
    for c in range(3):
        for i in range(25):
            IMP[0, pl.ds(25 * c + i, 1), :] = IM[pl.ds(8 * i, 1), :]
            IMP[1, pl.ds(25 * c + i, 1), :] = IM[pl.ds(8 * i + 4, 1), :]
    for i in range(75, ROWS):
        IMP[0, pl.ds(i, 1), :] = jnp.zeros((1, 128), f32)
        IMP[1, pl.ds(i, 1), :] = jnp.zeros((1, 128), f32)

    def wide(ref):
        z = jnp.zeros((1, 96), f32)
        out = jnp.zeros((8, 128), f32)
        for e in range(4):
            row = jnp.concatenate([ref[0, pl.ds(e, 1), :], z], axis=1)
            row = jnp.broadcast_to(row, (8, 128))
            out = jnp.where(blk == e, roll(row, 32 * e), out)
        return out

    wq = by_sub([w / 8.0 for w in W5])
    lam_x = wide(lamv) * wq
    mu_x = wide(muv) * wq
    for i, (a, b) in enumerate(WPAIR):
        w = float(W5[a] * W5[b])
        CONST[10 + i] = lam_x * w
        CONST[16 + i] = mu_x * w

    def planes(own, ghost):
        top = jnp.concatenate([own, jnp.zeros((4, 128), own.dtype)], axis=0)
        low = jnp.concatenate([ghost, ghost], axis=0)
        return jnp.where(sub == 4, low, top)

    def spread(ghost):
        return jnp.broadcast_to(ghost[0:1], (4, 128))

    live5 = live_x

    for i in range(STEPS):
        own_f = planes(flagv[i, 0], spread(gflag[0, i, 0]))
        low_f = planes(gflag[2, i, 0], spread(gflag[1, i, 0]))
        own_s = planes(slopev[0], spread(gslope[0, 0]))
        low_s = planes(gslope[2, 0], spread(gslope[1, 0]))
        for j, (fl, sl) in enumerate(((own_f, own_s), (low_f, low_s))):
            t = jnp.where(fl == 0, LOCK, jnp.where(fl == 1, -sl, 0.0))
            t = jnp.where(live5, t, 0.0)
            TH[j, i] = permute(t, to_packed)
        h = jnp.where(own_f == 1, 0.5, jnp.where(own_f == 2, 1.0, 0.0))
        stress = jnp.concatenate([nsv[0], jnp.zeros((4, 128), f32)], axis=0)
        TH[2, i] = permute(jnp.where(sub < 4, h * stress, 0.0), to_packed)

    grad[...] = jnp.zeros((8, 128), f32)

    def dom_copy(side, step):
        to = me - 1 if side == 0 else me + 1
        return pltpu.make_async_remote_copy(
            src_ref=send_dom.at[side, step],
            dst_ref=recv_dom.at[side, step],
            send_sem=dsend.at[side, step],
            recv_sem=drecv.at[side, step],
            device_id=(to, my),
            device_id_type=MESH,
        )

    def dep_copy(side, step):
        to = dn if side == 0 else up
        return pltpu.make_async_remote_copy(
            src_ref=send_dep.at[side, step],
            dst_ref=recv_dep.at[side, step],
            send_sem=fsend.at[side, step],
            recv_sem=frecv.at[side, step],
            device_id=(me, to),
            device_id_type=MESH,
        )

    def patch_copy(i):
        return pltpu.make_async_remote_copy(
            src_ref=psend.at[i],
            dst_ref=precv.at[i],
            send_sem=pss.at[i],
            recv_sem=prs.at[i],
            device_id=(me + OFFSETS[i], my),
            device_id_type=MESH,
        )

    def inside(v):
        return jnp.logical_and(v >= 0, v < nd)

    def step_body(step, carry):
        cur = lax.rem(step, 2)
        new = 1 - cur

        def u(c, yl, zl):
            return S[cur, pl.ds(8 * rblk(c, yl, zl), 8), :]

        for c in range(3):
            low = [roll(u(c, 0, z), 32 * z) for z in range(4)]
            high = [roll(u(c, 4, z), 32 * (z - 3)) for z in range(4)]
            send_dep[0, step, c] = pick(*low)
            send_dep[1, step, c] = pick(*high)
        dep_copy(0, step).start()
        dep_copy(1, step).start()

        for c in range(3):
            for zl in range(5):
                g = apply5(D5, [u(c, yl, zl) for yl in range(5)])
                for yl in range(5):
                    GY[pl.ds(8 * rblk(c, yl, zl), 8), :] = g[yl]
        for yl in range(5):
            gz = [apply5(D5, [u(c, yl, zl) for zl in range(5)]) for c in range(3)]
            fz = [[None] * 5 for _ in range(3)]
            for zl in range(5):
                gx, gy = [], []
                for c in range(3):
                    r = 8 * rblk(c, yl, zl)
                    acc = None
                    for k in range(5):
                        row = jnp.broadcast_to(S[cur, pl.ds(r + k, 1), :], (8, 128))
                        t = row * CONST[k]
                        acc = t if acc is None else acc + t
                    gx.append(acc)
                    gy.append(GY[pl.ds(r, 8), :])
                key = wkey(yl, zl)
                lw, mw = CONST[10 + key], CONST[16 + key]
                m2 = mw + mw
                common = lw * (gx[0] + gy[1] + gz[2][zl])
                sxx = common + m2 * gx[0]
                syy = common + m2 * gy[1]
                szz = common + m2 * gz[2][zl]
                sxy = mw * (gx[1] + gy[0])
                sxz = mw * (gx[2] + gz[0][zl])
                syz = mw * (gy[2] + gz[1][zl])
                for c, (vx, vy, vz) in enumerate(
                    ((sxx, sxy, sxz), (sxy, syy, syz), (sxz, syz, szz))
                ):
                    r = 8 * rblk(c, yl, zl)
                    FX[pl.ds(r, 8), :] = vx
                    FY[pl.ds(r, 8), :] = vy
                    fz[c][zl] = vz
            for c in range(3):
                back = apply5(D5.T, fz[c])
                for zl in range(5):
                    F[pl.ds(8 * rblk(c, yl, zl), 8), :] = back[zl]
        for c in range(3):
            for zl in range(5):
                rs = [8 * rblk(c, yl, zl) for yl in range(5)]
                back = apply5(D5.T, [FY[pl.ds(r, 8), :] for r in rs])
                for yl, r in enumerate(rs):
                    acc = back[yl] + F[pl.ds(r, 8), :]
                    for q in range(5):
                        row = jnp.broadcast_to(FX[pl.ds(r + q, 1), :], (8, 128))
                        acc = acc + row * CONST[5 + q]
                    F[pl.ds(r, 8), :] = acc

        for c in range(3):
            for yl in range(5):
                ra, rb = 8 * rblk(c, yl, 0), 8 * rblk(c, yl, 4)
                fa, fb = F[pl.ds(ra, 8), :], F[pl.ds(rb, 8), :]
                F[pl.ds(ra, 8), :] = fa + jnp.where(ez == 0, 0.0, roll(fb, 1))
                F[pl.ds(rb, 8), :] = fb + roll(fa, -1)
        for c in range(3):
            for zl in range(5):
                ra, rb = 8 * rblk(c, 0, zl), 8 * rblk(c, 4, zl)
                fa, fb = F[pl.ds(ra, 8), :], F[pl.ds(rb, 8), :]
                F[pl.ds(ra, 8), :] = fa + jnp.where(b0, 0.0, roll(fb, 32))
                F[pl.ds(rb, 8), :] = fb + jnp.where(b3, 0.0, roll(fa, -32))

        for g in range(ROWS // 8):
            send_dom[0, step, pl.ds(8 * g, 8), :] = F[pl.ds(64 * g, 8, stride=8), :]
            send_dom[1, step, pl.ds(8 * g, 8), :] = F[pl.ds(64 * g + 4, 8, stride=8), :]

        @pl.when(has_l)
        def _():
            dom_copy(0, step).start()

        @pl.when(has_r)
        def _():
            dom_copy(1, step).start()

        dep_copy(0, step).wait_recv()
        dep_copy(1, step).wait_recv()
        slip0 = None
        for c in range(3):
            slip_hi = recv_dep[0, step, c] - send_dep[1, step, c]
            slip_lo = send_dep[0, step, c] - recv_dep[1, step, c]
            if c == 0:
                slip0 = slip_hi
            t_hi = LOCK if c == 1 else TH[0, step]
            t_lo = LOCK if c == 1 else TH[1, step]
            hi = t_hi * slip_hi
            lo = t_lo * slip_lo
            for zl in range(5):
                sh = (96, 0) if zl < 4 else (95, -1)
                zb = zl if zl < 4 else 0
                rh, rl = 8 * rblk(c, 4, zl), 8 * rblk(c, 0, zl)
                F[pl.ds(rh, 8), :] = F[pl.ds(rh, 8), :] - jnp.where(
                    b3, roll(hi, sh[0] - 32 * zb), 0.0
                )
                F[pl.ds(rl, 8), :] = F[pl.ds(rl, 8), :] + jnp.where(
                    b0, roll(lo, sh[1] - 32 * zb), 0.0
                )
        grad[...] = grad[...] + TH[2, step] * slip0

        for yl in range(5):
            for zl in range(5):
                im = IM[pl.ds(8 * (yl * 5 + zl), 8), :]
                for c in range(3):
                    r = pl.ds(8 * rblk(c, yl, zl), 8)
                    now_u = S[cur, r, :]
                    S[new, r, :] = (now_u + now_u) - S[new, r, :] - im * F[r, :]

        def add_side(side, first):
            for g in range(ROWS // 8):
                r = pl.ds(64 * g + first, 8, stride=8)
                d = pl.ds(8 * g, 8)
                plane = 0 if first == 0 else 1
                S[new, r, :] = S[new, r, :] - IMP[plane, d, :] * recv_dom[side, step, d, :]

        @pl.when(has_l)
        def _():
            dom_copy(1, step).wait_recv()
            add_side(1, 0)

        @pl.when(has_r)
        def _():
            dom_copy(0, step).wait_recv()
            add_side(0, 4)

        return carry

    lax.fori_loop(0, STEPS, step_body, 0)

    total = permute(grad[...], to_natural)
    rows = [total[x : x + 1] for x in range(4)]

    def members(off, p):
        num = (me + off) * 2 + p
        acc = jnp.zeros((1, 128), f32)
        for x in range(4):
            acc = acc + jnp.where(ownv[0, x] == num, rows[x], 0.0)
        return acc

    for i, off in enumerate(OFFSETS):
        psend[i] = jnp.zeros((8, 128), f32)
        for p in range(2):
            psend[i, pl.ds(p, 1), :] = members(off, p)

        @pl.when(inside(me + off))
        def _(i=i):
            patch_copy(i).start()

    patchv[0, pl.ds(0, 1), :] = members(0, 0)
    patchv[0, pl.ds(1, 1), :] = members(0, 1)

    def from_elements(slot, which, out):
        for c in range(3):
            def e(yl, zl):
                return S[slot, pl.ds(8 * rblk(c, yl, zl), 8), :]

            for y in range(17):
                ey, yl = (y // 4, y % 4) if y < 16 else (3, 4)
                v = pick(*[roll(e(yl, zl), 32 * (zl - ey)) for zl in range(4)])
                stage[pl.ds(c * 192 + y, 8, stride=24), :] = permute(v, to_natural)
        for c in range(3):
            for x in range(4):
                outv[which, c, x] = stage[pl.ds((c * 8 + x) * 24, 17), :]
        cp = pltpu.make_async_copy(outv.at[which], out, osem.at[which])
        cp.start()
        return cp

    cps = [from_elements(STEPS % 2, 0, out_cur), from_elements(1 - STEPS % 2, 1, out_fol)]

    for i, off in enumerate(OFFSETS):

        @pl.when(inside(me - off))
        def _(i=i):
            patch_copy(i).wait_recv()
            patchv[0] = patchv[0] + precv[i, pl.ds(0, 2), :]

    cp = pltpu.make_async_copy(patchv, out_patch, osem.at[2])
    cp.start()
    cps.append(cp)

    @pl.when(has_l)
    def _():
        for cp in to_left:
            cp.wait_send()
        for s in range(STEPS):
            dom_copy(0, s).wait_send()

    @pl.when(has_r)
    def _():
        for s in range(STEPS):
            dom_copy(1, s).wait_send()

    for cp in to_up:
        cp.wait_send()
    for s in range(STEPS):
        dep_copy(0, s).wait_send()
        dep_copy(1, s).wait_send()
    for i, off in enumerate(OFFSETS):

        @pl.when(inside(me + off))
        def _(i=i):
            patch_copy(i).wait_send()

    for cp in cps:
        cp.wait()


def solution(mesh):
    nd, ndp = mesh.shape["dom"], mesh.shape["depth"]

    def on_device(now, nxt, lam, mu, dens, flags, slope, ns, owner):
        any_ = pl.BlockSpec(memory_space=pl.ANY)
        dma = pltpu.SemaphoreType.DMA
        vm = pltpu.VMEM
        i32 = jnp.int32
        return pl.pallas_call(
            functools.partial(kernel, nd, ndp),
            name="rupture",
            out_shape=(
                jax.ShapeDtypeStruct((3, 4, 17, 128), f32),
                jax.ShapeDtypeStruct((3, 4, 17, 128), f32),
                jax.ShapeDtypeStruct((1, 2, 128), f32),
            ),
            in_specs=[any_] * 9,
            out_specs=[any_] * 3,
            scratch_shapes=[
                vm((3, 4, 17, 128), f32),
                vm((3, 4, 17, 128), f32),
                vm((4, 17, 128), f32),
                vm((1, 4, 32), f32),
                vm((1, 4, 32), f32),
                vm((4, 1, 4, 128), i32),
                vm((1, 4, 128), f32),
                vm((1, 4, 128), f32),
                pltpu.SMEM((1, 4), i32),
                vm((3, 17, 128), f32),
                vm((3, 17, 128), f32),
                vm((17, 128), f32),
                vm((3, 4, 1, 4, 128), i32),
                vm((3, 1, 4, 128), f32),
                vm((3 * 8 * 24, 128), f32),
                vm((2, ROWS * 8, 128), f32),
                vm((ROWS * 8, 128), f32),
                vm((ROWS * 8, 128), f32),
                vm((ROWS * 8, 128), f32),
                vm((ROWS * 8, 128), f32),
                vm((25 * 8, 128), f32),
                vm((2, ROWS, 128), f32),
                vm((22, 8, 128), f32),
                vm((3, STEPS, 8, 128), f32),
                vm((8, 128), f32),
                vm((2, STEPS, ROWS, 128), f32),
                vm((2, STEPS, ROWS, 128), f32),
                vm((2, STEPS, 3, 8, 128), f32),
                vm((2, STEPS, 3, 8, 128), f32),
                vm((4, 8, 128), f32),
                vm((4, 8, 128), f32),
                vm((2, 3, 4, 17, 128), f32),
                vm((1, 2, 128), f32),
                dma((9,)),
                dma((9,)),
                dma((9,)),
                dma((2, STEPS)),
                dma((2, STEPS)),
                dma((2, STEPS)),
                dma((2, STEPS)),
                dma((4,)),
                dma((4,)),
                dma((3,)),
            ],
            compiler_params=pltpu.CompilerParams(collective_id=0, has_side_effects=True),
        )(now, nxt, lam, mu, dens, flags, slope, ns, owner)

    return jax.shard_map(
        on_device,
        mesh=mesh,
        in_specs=(
            P(None, "dom", "depth", None),
            P(None, "dom", "depth", None),
            P("dom", "depth", None),
            P("dom", "depth", None),
            P("dom", "depth", None),
            P(None, "depth", "dom", None),
            P("depth", "dom", None),
            P("depth", "dom", None),
            P("depth", "dom"),
        ),
        out_specs=(
            P(None, "dom", "depth", None),
            P(None, "dom", "depth", None),
            P("depth", "dom", None),
        ),
        check_vma=False,
    )
```

profile of v0, /device:TPU:32, one launch (start us, length us, event | category | flops | bytes accessed | tf_op | source)
XLA Modules:
  0.0 53.7 jit_solution(11129203364770289128)
XLA Ops:
  0.6 1.4 %copy.14.dens = f32[4,17,128]{2,1,0:T(8,128)} copy(f32[4,17,128]{2,0,1:T(4,128)} %param.13) | data formatting | bytes 69632 | tf_op args[4]
  2.0 0.0 copy-start.1
  2.0 1.6 %copy.12.now = f32[3,4,17,128]{3,2,1,0:T(8,128)} copy(f32[3,4,17,128]{3,1,2,0:T(4,128)} %param.9) | data formatting | bytes 208896 | tf_op args[0]
  3.6 0.0 copy-done.1
  3.6 0.7 %copy.13.nxt = f32[3,4,17,128]{3,2,1,0:T(8,128)} copy(f32[3,4,17,128]{3,1,2,0:T(4,128)S(1)} %copy-done.1) | data formatting | bytes 208896 | tf_op args[1]
  4.3 46.5 %rupture.1 = (f32[3,4,17,128]{3,2,1,0:T(8,128)}, f32[3,4,17,128]{3,2,1,0:T(8,128)}, f32[1,2,128]{2,1,0:T(2,128)}) custom-call(f32[3,4,17,128]{3,2,1,0:T(8,128)} %copy.12.now, f32[3,4,17,128]{3,2,1,0:T(8,128)} %copy.13.nxt, f32[1,4,32]{2,1,0:T(4,128)} %lam.1, f32[1,4,32]{2,1,0:T(4,128)} %mu.1, f32[4,17,128]{2,1,0:T(8,128)} %copy.14.dens, ...), custom_call_target="tpu_custom_call" | custom-call | tf_op jit(solution)/shard_map/rupture/pallas_call | solution.py:617
  50.8 0.0 copy-start
  50.8 1.6 %copy.15 = f32[3,4,17,128]{3,1,2,0:T(4,128)} copy(f32[3,4,17,128]{3,2,1,0:T(8,128)} %get-tuple-element.3) | data formatting | bytes 208896 | tf_op jit(solution)/shard_map/rupture/pallas_call | solution.py:617
  52.4 0.0 copy-done
  52.4 0.0 copy-start.2
  52.4 0.7 %copy.16 = f32[3,4,17,128]{3,1,2,0:T(4,128)} copy(f32[3,4,17,128]{3,2,1,0:T(8,128)S(1)} %copy-done) | data formatting | bytes 208896 | tf_op jit(solution)/shard_map/rupture/pallas_call | solution.py:617
  53.1 0.0 copy-done.2
  53.1 0.6 %copy.18 = f32[1,2,128]{2,1,0:T(2,128)} copy(f32[1,2,128]{2,1,0:T(2,128)S(1)} %copy-done.2) | data formatting | bytes 2048
Async XLA Ops:
  2.0 1.6 %copy-start.1 = (f32[3,4,17,128]{3,1,2,0:T(4,128)S(1)}, f32[3,4,17,128]{3,1,2,0:T(4,128)}, u32[]{:S(2)}) copy-start(f32[3,4,17,128]{3,1,2,0:T(4,128)} %param.10) | copy-start | bytes 313348
  50.8 1.6 %copy-start = (f32[3,4,17,128]{3,2,1,0:T(8,128)S(1)}, f32[3,4,17,128]{3,2,1,0:T(8,128)}, u32[]{:S(2)}) copy-start(f32[3,4,17,128]{3,2,1,0:T(8,128)} %get-tuple-element.4) | copy-start | bytes 313348
  52.4 0.7 %copy-start.2 = (f32[1,2,128]{2,1,0:T(2,128)S(1)}, f32[1,2,128]{2,1,0:T(2,128)}, u32[]{:S(2)}) copy-start(f32[1,2,128]{2,1,0:T(2,128)} %get-tuple-element.11) | copy-start | bytes 3076
where the time goes:
time: 54.2 us; the launch traced here: 53.7 us
  Pallas kernels  46.5 us (86%)
  local copies, waits for them, and re-layouts  6.52 us (12%)
  between operations  0.65 us (1%)
    pallas_call x1, Pallas kernels, on_device(): pl.pallas_call(functools.partial(kernel, nd, ndp), name='rupture', out_sh...  46.5 us
    unnamed x10, local copies, waits for them, and re-layouts  4.23 us
    pallas_call x2, local copies, waits for them, and re-layouts, on_device(): pl.pallas_call(functools.partial(kernel, nd, ndp), name='rupture', out_sh...  2.29 us

commit v1 on v0

v1 whole, which is shorter than its diff:
```python
import functools
import math

import jax
import jax.numpy as jnp
import numpy as np
from jax import lax
from jax.experimental import pallas as pl
from jax.experimental.pallas import tpu as pltpu
from jax.sharding import PartitionSpec as P


MESH = pl.DeviceIdType.MESH
STEPS = 4
ROWS = 80
DT2 = 0.01 * 0.01
LOCK = 0.5
W5 = [0.1, 49.0 / 90.0, 32.0 / 45.0, 49.0 / 90.0, 0.1]
OFFSETS = (-2, -1, 1, 2)
f32 = jnp.float32


def slopes5():
    pts = [-1.0, -math.sqrt(3.0 / 7.0), 0.0, math.sqrt(3.0 / 7.0), 1.0]
    prod = [np.prod([pts[a] - pts[b] for b in range(5) if b != a]) for a in range(5)]
    d = np.zeros((5, 5))
    for a in range(5):
        for b in range(5):
            if a == b:
                d[a, b] = sum(1.0 / (pts[a] - pts[o]) for o in range(5) if o != a)
            else:
                d[a, b] = prod[a] / prod[b] / (pts[a] - pts[b])
    d[2, 2] = 0.0
    return 2.0 * d


D5 = slopes5()


def apply5(m, v):
    e0, e1, o0, o1 = v[0] + v[4], v[1] + v[3], v[0] - v[4], v[1] - v[3]
    out = [None] * 5
    for q in (0, 1):
        a = (
            float((m[q, 0] + m[q, 4]) / 2) * e0
            + float((m[q, 1] + m[q, 3]) / 2) * e1
            + float(m[q, 2]) * v[2]
        )
        b = float((m[q, 0] - m[q, 4]) / 2) * o0 + float((m[q, 1] - m[q, 3]) / 2) * o1
        out[q] = b + a
        out[4 - q] = b - a
    out[2] = float((m[2, 0] - m[2, 4]) / 2) * o0 + float((m[2, 1] - m[2, 3]) / 2) * o1
    return out


def wkey(a, b):
    a, b = min(a, 4 - a), min(b, 4 - b)
    a, b = min(a, b), max(a, b)
    return {(0, 0): 0, (0, 1): 1, (0, 2): 2, (1, 1): 3, (1, 2): 4, (2, 2): 5}[(a, b)]


WPAIR = [(0, 0), (0, 1), (0, 2), (1, 1), (1, 2), (2, 2)]


def rblk(c, yl, zl):
    return (c * 5 + yl) * 5 + zl


def kernel(
    nd,
    ndp,
    now,
    nxt,
    lam,
    mu,
    dens,
    flags,
    slope,
    ns,
    owner,
    out_cur,
    out_fol,
    out_patch,
    nowv,
    nxtv,
    densv,
    modv,
    flagv,
    slopev,
    nsv,
    ownv,
    gflag,
    gslope,
    S,
    F,
    GY,
    FX,
    FY,
    IM,
    IMP,
    CONST,
    TH,
    grad,
    send_dom,
    recv_dom,
    send_dep,
    recv_dep,
    psend,
    precv,
    outv,
    patchv,
    lsem,
    isend,
    irecv,
    dsend,
    drecv,
    fsend,
    frecv,
    pss,
    prs,
    osem,
):
    me = lax.axis_index("dom")
    my = lax.axis_index("depth")
    up = lax.rem(my + 1, ndp)
    dn = lax.rem(my + ndp - 1, ndp)
    has_l = me > 0
    has_r = me < nd - 1
    odd = lax.rem(me, 2) == 1

    barrier = pltpu.get_barrier_semaphore()
    count = 2
    for off, row in ((-1, my), (1, my), (-2, my), (2, my), (-1, up), (1, dn)):
        ok = jnp.logical_and(me + off >= 0, me + off < nd)
        count = count + ok.astype(jnp.int32)

        @pl.when(ok)
        def _(off=off, row=row):
            pl.semaphore_signal(
                barrier, inc=1, device_id=(me + off, row), device_id_type=MESH
            )

    pl.semaphore_signal(barrier, inc=1, device_id=(me, up), device_id_type=MESH)
    pl.semaphore_signal(barrier, inc=1, device_id=(me, dn), device_id_type=MESH)

    locals_ = [
        pltpu.make_async_copy(a, b, lsem.at[i])
        for i, (a, b) in enumerate(
            [
                (now, nowv.at[0, :, :, 0:4, :]),
                (now.at[:, :, 0:1, :], nowv.at[1, :, :, 4:5, :]),
                (lam, modv.at[0, 0]),
                (mu, modv.at[0, 1]),
                (nxt, nxtv.at[:, :, 0:4, :]),
                (dens, densv.at[:, 0:4, :]),
                (flags, flagv),
                (slope, slopev),
                (ns, nsv),
                (owner, ownv),
            ]
        )
    ]
    for cp in locals_:
        cp.start()
    pl.semaphore_wait(barrier, count)

    def remote(i, src, dst, to):
        return pltpu.make_async_remote_copy(
            src_ref=src,
            dst_ref=dst,
            send_sem=isend.at[i],
            recv_sem=irecv.at[i],
            device_id=to,
            device_id_type=MESH,
        )

    to_left = [
        remote(0, now.at[:, :, 0:1, :], nowv.at[0, :, :, 4:5, :], (me - 1, my)),
        remote(1, nxt.at[:, :, 0:1, :], nxtv.at[:, :, 4:5, :], (me - 1, my)),
        remote(2, dens.at[:, 0:1, :], densv.at[:, 4:5, :], (me - 1, my)),
        remote(3, flags, gflag.at[0], (me - 1, my)),
        remote(4, slope, gslope.at[0], (me - 1, my)),
        remote(5, flags, gflag.at[1], (me - 1, up)),
        remote(6, slope, gslope.at[1], (me - 1, up)),
    ]
    to_up = [
        remote(7, flags, gflag.at[2], (me, up)),
        remote(8, slope, gslope.at[2], (me, up)),
    ]
    to_right = [
        remote(9, now, nowv.at[1, :, :, 0:4, :], (me + 1, my)),
        remote(10, lam, modv.at[1, 0], (me + 1, my)),
        remote(11, mu, modv.at[1, 1], (me + 1, my)),
    ]

    @pl.when(has_l)
    def _():
        to_left[0].start()

    @pl.when(has_r)
    def _():
        for cp in to_right:
            cp.start()

    @pl.when(has_l)
    def _():
        for cp in to_left[1:]:
            cp.start()

    for cp in to_up:
        cp.start()

    lane = lax.broadcasted_iota(jnp.int32, (8, 128), 1)
    sub = lax.broadcasted_iota(jnp.int32, (8, 128), 0)
    blk = lane // 32
    ez = lane % 32
    to_packed = 4 * ez + blk
    to_natural = (lane % 4) * 32 + lane // 4
    b0, b1, b2, b3 = blk == 0, blk == 1, blk == 2, blk == 3

    def permute(x, idx):
        return jnp.take_along_axis(x, idx, axis=1)

    def roll(x, shift):
        shift = shift % 128
        return x if shift == 0 else pltpu.roll(x, shift, 1)

    def by_sub(vals):
        v = jnp.full((8, 128), 0.0, f32)
        for i, x in enumerate(vals):
            if x != 0.0:
                v = jnp.where(sub == i, float(x), v)
        return v

    for k in range(5):
        CONST[k] = by_sub(D5[:, k])
        CONST[5 + k] = by_sub(D5[k, :])

    for i in range(75, ROWS):
        for slot in range(2):
            F[slot, pl.ds(8 * i, 8), :] = jnp.zeros((8, 128), f32)
            S[slot, pl.ds(8 * i, 8), :] = jnp.zeros((8, 128), f32)

    live_x = jnp.logical_or(sub < 4, jnp.logical_and(sub == 4, has_r))

    def pick(r0, r1, r2, r3):
        return jnp.where(b0, r0, jnp.where(b1, r1, jnp.where(b2, r2, r3)))

    def to_elements(load, put, bottom):
        packed = [permute(load(y), to_packed) for y in range(17)]
        rolled = [[roll(v, 32 * s) for s in range(4)] for v in packed]
        for yl in range(5):
            for zl in range(4):
                v = pick(*[rolled[4 * e + yl][(e - zl) % 4] for e in range(4)])
                put(yl, zl, v)
                if zl == 0:
                    first = v
            put(yl, 4, jnp.where(ez == 31, bottom, roll(first, -1)))

    def wide(slot, which):
        z = jnp.zeros((1, 96), f32)
        out = jnp.zeros((8, 128), f32)
        for e in range(4):
            row = jnp.concatenate([modv[slot, which, 0, pl.ds(e, 1), :], z], axis=1)
            row = jnp.broadcast_to(row, (8, 128))
            out = jnp.where(blk == e, roll(row, 32 * e), out)
        return out

    def put_moduli(slot):
        wq = by_sub([w / 8.0 for w in W5])
        for j in range(2):
            m = wide(slot, j) * wq
            for i, (a, b) in enumerate(WPAIR):
                CONST[10 + 12 * slot + 6 * j + i] = m * float(W5[a] * W5[b])

    def mass_table():
        wx = by_sub([0.2, W5[1], W5[2], W5[3], 0.2])
        wx = jnp.where(sub == 0, jnp.where(has_l, 0.2, 0.1), wx)

        def put_mass(yl, zl, v):
            if yl in (1, 2, 3):
                wy = W5[yl]
            else:
                wy = jnp.where(b0 if yl == 0 else b3, 0.1, 0.2)
            if zl in (1, 2, 3):
                wz = W5[zl]
            elif zl == 0:
                wz = jnp.where(ez == 0, 0.1, 0.2)
            else:
                wz = 0.2
            mass = v * wx * wy * wz
            live = jnp.logical_and(live_x, ez < 31) if zl == 4 else live_x
            IM[pl.ds(8 * (yl * 5 + zl), 8), :] = jnp.where(
                live, (8.0 * DT2) / jnp.where(live, mass, 1.0), 0.0
            )

        to_elements(lambda y: jnp.where(live_x, densv[y], 1.0), put_mass, 1.0)
        for c in range(3):
            for i in range(25):
                IMP[0, pl.ds(25 * c + i, 1), :] = IM[pl.ds(8 * i, 1), :]
                IMP[1, pl.ds(25 * c + i, 1), :] = IM[pl.ds(8 * i + 4, 1), :]
        for i in range(75, ROWS):
            IMP[0, pl.ds(i, 1), :] = jnp.zeros((1, 128), f32)
            IMP[1, pl.ds(i, 1), :] = jnp.zeros((1, 128), f32)

    def following_field():
        for c in range(3):

            def put(yl, zl, v, c=c):
                S[1, pl.ds(8 * rblk(c, yl, zl), 8), :] = v

            to_elements(lambda y, c=c: jnp.where(live_x, nxtv[c, y], 0.0), put, 0.0)

    def fault_tables():
        def planes(own, ghost):
            top = jnp.concatenate([own, jnp.zeros((4, 128), own.dtype)], axis=0)
            low = jnp.concatenate([ghost, ghost], axis=0)
            return jnp.where(sub == 4, low, top)

        def spread(ghost):
            return jnp.broadcast_to(ghost[0:1], (4, 128))

        own_s = planes(slopev[0], spread(gslope[0, 0]))
        low_s = planes(gslope[2, 0], spread(gslope[1, 0]))
        stress = jnp.concatenate([nsv[0], jnp.zeros((4, 128), f32)], axis=0)
        for i in range(STEPS):
            own_f = planes(flagv[i, 0], spread(gflag[0, i, 0]))
            low_f = planes(gflag[2, i, 0], spread(gflag[1, i, 0]))
            for j, (fl, sl) in enumerate(((own_f, own_s), (low_f, low_s))):
                t = jnp.where(fl == 0, LOCK, jnp.where(fl == 1, -sl, 0.0))
                TH[j, i] = permute(jnp.where(live_x, t, 0.0), to_packed)
            h = jnp.where(own_f == 1, 0.5, jnp.where(own_f == 2, 1.0, 0.0))
            TH[2, i] = permute(jnp.where(sub < 4, h * stress, 0.0), to_packed)

    def dom_copy(side, step):
        to = me - 1 if side == 0 else me + 1
        return pltpu.make_async_remote_copy(
            src_ref=send_dom.at[side, step],
            dst_ref=recv_dom.at[side, step],
            send_sem=dsend.at[side, step],
            recv_sem=drecv.at[side, step],
            device_id=(to, my),
            device_id_type=MESH,
        )

    def dep_copy(side, step):
        to = dn if side == 0 else up
        return pltpu.make_async_remote_copy(
            src_ref=send_dep.at[side, step],
            dst_ref=recv_dep.at[side, step],
            send_sem=fsend.at[side, step],
            recv_sem=frecv.at[side, step],
            device_id=(me, to),
            device_id_type=MESH,
        )

    def patch_copy(i):
        return pltpu.make_async_remote_copy(
            src_ref=psend.at[i],
            dst_ref=precv.at[i],
            send_sem=pss.at[i],
            recv_sem=prs.at[i],
            device_id=(me + OFFSETS[i], my),
            device_id_type=MESH,
        )

    def inside(v):
        return jnp.logical_and(v >= 0, v < nd)

    def send_patches():
        total = permute(grad[...], to_natural)
        rows = [total[x : x + 1] for x in range(4)]

        def members(off, p):
            num = (me + off) * 2 + p
            acc = jnp.zeros((1, 128), f32)
            for x in range(4):
                acc = acc + jnp.where(ownv[0, x] == num, rows[x], 0.0)
            return acc

        for i, off in enumerate(OFFSETS):
            psend[i] = jnp.zeros((8, 128), f32)
            for p in range(2):
                psend[i, pl.ds(p, 1), :] = members(off, p)

            @pl.when(inside(me + off))
            def _(i=i):
                patch_copy(i).start()

        patchv[0, pl.ds(0, 1), :] = members(0, 0)
        patchv[0, pl.ds(1, 1), :] = members(0, 1)

    out_copies = [
        pltpu.make_async_copy(outv.at[0, :, :, 0:4, :], out_cur, osem.at[0]),
        pltpu.make_async_copy(outv.at[1, :, :, 0:4, :], out_fol, osem.at[1]),
        pltpu.make_async_copy(patchv, out_patch, osem.at[2]),
    ]

    def from_elements(slot, which):
        for c in range(3):

            def e(yl, zl):
                return S[slot, pl.ds(8 * rblk(c, yl, zl), 8), :]

            for y in range(17):
                ey, yl = (y // 4, y % 4) if y < 16 else (3, 4)
                v = pick(*[roll(e(yl, zl), 32 * (zl - ey)) for zl in range(4)])
                outv[which, c, y] = permute(v, to_natural)
        out_copies[which].start()

    grad[...] = jnp.zeros((8, 128), f32)

    def turn(it, carry):
        step = jnp.maximum(it - 1, 0)
        is_left = jnp.logical_or(
            jnp.logical_and(it == 0, odd),
            jnp.logical_and(it == 1, jnp.logical_not(odd)),
        )
        own = jnp.logical_not(is_left)
        cur = lax.rem(step, 2)
        new = 1 - cur
        fs = is_left.astype(jnp.int32)
        src = cur + 2 * fs
        cb = 10 + 12 * fs

        @pl.when(it < 2)
        def _():
            @pl.when(is_left)
            def _():
                locals_[1].wait()

                @pl.when(has_l)
                def _():
                    for cp in to_right:
                        cp.wait_recv()

                put_moduli(1)

            @pl.when(own)
            def _():
                for cp in (locals_[0], locals_[2], locals_[3]):
                    cp.wait()
                put_moduli(0)

                @pl.when(has_r)
                def _():
                    to_left[0].wait_recv()

            live = jnp.logical_or(
                sub < 4, jnp.logical_and(sub == 4, jnp.logical_or(is_left, has_r))
            )
            for c in range(3):

                def put(yl, zl, v, c=c):
                    S[src, pl.ds(8 * rblk(c, yl, zl), 8), :] = v

                to_elements(
                    lambda y, c=c: jnp.where(live, nowv[fs, c, y], 0.0), put, 0.0
                )

        def u(c, yl, zl):
            return S[src, pl.ds(8 * rblk(c, yl, zl), 8), :]

        @pl.when(own)
        def _():
            for c in range(3):
                low = [roll(u(c, 0, z), 32 * z) for z in range(4)]
                high = [roll(u(c, 4, z), 32 * (z - 3)) for z in range(4)]
                send_dep[0, step, c] = pick(*low)
                send_dep[1, step, c] = pick(*high)
            dep_copy(0, step).start()
            dep_copy(1, step).start()

        for c in range(3):
            for zl in range(5):
                g = apply5(D5, [u(c, yl, zl) for yl in range(5)])
                for yl in range(5):
                    GY[pl.ds(8 * rblk(c, yl, zl), 8), :] = g[yl]
        for yl in range(5):
            gz = [apply5(D5, [u(c, yl, zl) for zl in range(5)]) for c in range(3)]
            fz = [[None] * 5 for _ in range(3)]
            for zl in range(5):
                gx, gy = [], []
                for c in range(3):
                    r = 8 * rblk(c, yl, zl)
                    acc = None
                    for k in range(5):
                        row = jnp.broadcast_to(S[src, pl.ds(r + k, 1), :], (8, 128))
                        t = row * CONST[k]
                        acc = t if acc is None else acc + t
                    gx.append(acc)
                    gy.append(GY[pl.ds(r, 8), :])
                key = wkey(yl, zl)
                lw, mw = CONST[cb + key], CONST[cb + 6 + key]
                m2 = mw + mw
                common = lw * (gx[0] + gy[1] + gz[2][zl])
                sxx = common + m2 * gx[0]
                syy = common + m2 * gy[1]
                szz = common + m2 * gz[2][zl]
                sxy = mw * (gx[1] + gy[0])
                sxz = mw * (gx[2] + gz[0][zl])
                syz = mw * (gy[2] + gz[1][zl])
                for c, (vx, vy, vz) in enumerate(
                    ((sxx, sxy, sxz), (sxy, syy, syz), (sxz, syz, szz))
                ):
                    r = 8 * rblk(c, yl, zl)
                    FX[pl.ds(r, 8), :] = vx
                    FY[pl.ds(r, 8), :] = vy
                    fz[c][zl] = vz
            for c in range(3):
                back = apply5(D5.T, fz[c])
                for zl in range(5):
                    F[fs, pl.ds(8 * rblk(c, yl, zl), 8), :] = back[zl]
        for c in range(3):
            for zl in range(5):
                rs = [8 * rblk(c, yl, zl) for yl in range(5)]
                back = apply5(D5.T, [FY[pl.ds(r, 8), :] for r in rs])
                for yl, r in enumerate(rs):
                    acc = back[yl] + F[fs, pl.ds(r, 8), :]
                    for q in range(5):
                        row = jnp.broadcast_to(FX[pl.ds(r + q, 1), :], (8, 128))
                        acc = acc + row * CONST[5 + q]
                    F[fs, pl.ds(r, 8), :] = acc

        for c in range(3):
            for yl in range(5):
                ra, rb = pl.ds(8 * rblk(c, yl, 0), 8), pl.ds(8 * rblk(c, yl, 4), 8)
                fa, fb = F[fs, ra, :], F[fs, rb, :]
                F[fs, ra, :] = fa + jnp.where(ez == 0, 0.0, roll(fb, 1))
                F[fs, rb, :] = fb + roll(fa, -1)
        for c in range(3):
            for zl in range(5):
                ra, rb = pl.ds(8 * rblk(c, 0, zl), 8), pl.ds(8 * rblk(c, 4, zl), 8)
                fa, fb = F[fs, ra, :], F[fs, rb, :]
                F[fs, ra, :] = fa + jnp.where(b0, 0.0, roll(fb, 32))
                F[fs, rb, :] = fb + jnp.where(b3, 0.0, roll(fa, -32))

        @pl.when(is_left)
        def _():
            for g in range(ROWS // 8):
                recv_dom[1, 0, pl.ds(8 * g, 8), :] = F[1, pl.ds(64 * g + 4, 8, stride=8), :]

        @pl.when(own)
        def _():
            for g in range(ROWS // 8):
                d = pl.ds(8 * g, 8)
                send_dom[0, step, d, :] = F[0, pl.ds(64 * g, 8, stride=8), :]
                send_dom[1, step, d, :] = F[0, pl.ds(64 * g + 4, 8, stride=8), :]

            @pl.when(has_l)
            def _():
                dom_copy(0, step).start()

            @pl.when(jnp.logical_and(has_r, step > 0))
            def _():
                dom_copy(1, step).start()

        @pl.when(it == 1)
        def _():
            for cp in locals_[4:]:
                cp.wait()
            for cp in to_up:
                cp.wait_recv()

            @pl.when(has_r)
            def _():
                for cp in to_left[1:]:
                    cp.wait_recv()

            following_field()
            mass_table()
            fault_tables()

        @pl.when(it > 0)
        def _():
            dep_copy(0, step).wait_recv()
            dep_copy(1, step).wait_recv()
            for c in range(3):
                slip_hi = recv_dep[0, step, c] - send_dep[1, step, c]
                slip_lo = send_dep[0, step, c] - recv_dep[1, step, c]
                if c == 0:
                    grad[...] = grad[...] + TH[2, step] * slip_hi
                hi = (LOCK if c == 1 else TH[0, step]) * slip_hi
                lo = (LOCK if c == 1 else TH[1, step]) * slip_lo
                for zl in range(5):
                    sh = (96, 0) if zl < 4 else (95, -1)
                    zb = zl if zl < 4 else 0
                    rh, rl = pl.ds(8 * rblk(c, 4, zl), 8), pl.ds(8 * rblk(c, 0, zl), 8)
                    F[0, rh, :] = F[0, rh, :] - jnp.where(
                        b3, roll(hi, sh[0] - 32 * zb), 0.0
                    )
                    F[0, rl, :] = F[0, rl, :] + jnp.where(
                        b0, roll(lo, sh[1] - 32 * zb), 0.0
                    )

            for yl in range(5):
                for zl in range(5):
                    im = IM[pl.ds(8 * (yl * 5 + zl), 8), :]
                    for c in range(3):
                        r = pl.ds(8 * rblk(c, yl, zl), 8)
                        now_u = S[cur, r, :]
                        S[new, r, :] = (now_u + now_u) - S[new, r, :] - im * F[0, r, :]

            @pl.when(it == STEPS)
            def _():
                send_patches()
                from_elements(1 - STEPS % 2, 1)

            def add_side(side, first):
                plane = 0 if first == 0 else 1
                for g in range(ROWS // 8):
                    r = pl.ds(64 * g + first, 8, stride=8)
                    d = pl.ds(8 * g, 8)
                    S[new, r, :] = S[new, r, :] - IMP[plane, d, :] * recv_dom[side, step, d, :]

            @pl.when(has_r)
            def _():
                dom_copy(0, step).wait_recv()
                add_side(0, 4)

            @pl.when(has_l)
            def _():
                @pl.when(step > 0)
                def _():
                    dom_copy(1, step).wait_recv()

                add_side(1, 0)

        return carry

    lax.fori_loop(0, STEPS + 1, turn, 0)

    from_elements(STEPS % 2, 0)
    for i, off in enumerate(OFFSETS):

        @pl.when(inside(me - off))
        def _(i=i):
            patch_copy(i).wait_recv()
            patchv[0] = patchv[0] + precv[i, pl.ds(0, 2), :]

    out_copies[2].start()

    @pl.when(has_l)
    def _():
        for cp in to_left:
            cp.wait_send()
        for s in range(STEPS):
            dom_copy(0, s).wait_send()

    @pl.when(has_r)
    def _():
        for cp in to_right:
            cp.wait_send()
        for s in range(1, STEPS):
            dom_copy(1, s).wait_send()

    for cp in to_up:
        cp.wait_send()
    for s in range(STEPS):
        dep_copy(0, s).wait_send()
        dep_copy(1, s).wait_send()
    for i, off in enumerate(OFFSETS):

        @pl.when(inside(me + off))
        def _(i=i):
            patch_copy(i).wait_send()

    for cp in out_copies:
        cp.wait()


def solution(mesh):
    nd, ndp = mesh.shape["dom"], mesh.shape["depth"]

    def on_device(now, nxt, lam, mu, dens, flags, slope, ns, owner):
        any_ = pl.BlockSpec(memory_space=pl.ANY)
        dma = pltpu.SemaphoreType.DMA
        vm = pltpu.VMEM
        i32 = jnp.int32
        cur, fol, patch = pl.pallas_call(
            functools.partial(kernel, nd, ndp),
            name="rupture",
            out_shape=(
                jax.ShapeDtypeStruct((3, 17, 4, 128), f32),
                jax.ShapeDtypeStruct((3, 17, 4, 128), f32),
                jax.ShapeDtypeStruct((1, 2, 128), f32),
            ),
            in_specs=[any_] * 9,
            out_specs=[any_] * 3,
            scratch_shapes=[
                vm((2, 3, 17, 8, 128), f32),
                vm((3, 17, 8, 128), f32),
                vm((17, 8, 128), f32),
                vm((2, 2, 1, 4, 32), f32),
                vm((4, 1, 4, 128), i32),
                vm((1, 4, 128), f32),
                vm((1, 4, 128), f32),
                pltpu.SMEM((1, 4), i32),
                vm((3, 4, 1, 4, 128), i32),
                vm((3, 1, 4, 128), f32),
                vm((3, ROWS * 8, 128), f32),
                vm((2, ROWS * 8, 128), f32),
                vm((ROWS * 8, 128), f32),
                vm((ROWS * 8, 128), f32),
                vm((ROWS * 8, 128), f32),
                vm((25 * 8, 128), f32),
                vm((2, ROWS, 128), f32),
                vm((34, 8, 128), f32),
                vm((3, STEPS, 8, 128), f32),
                vm((8, 128), f32),
                vm((2, STEPS, ROWS, 128), f32),
                vm((2, STEPS, ROWS, 128), f32),
                vm((2, STEPS, 3, 8, 128), f32),
                vm((2, STEPS, 3, 8, 128), f32),
                vm((4, 8, 128), f32),
                vm((4, 8, 128), f32),
                vm((2, 3, 17, 8, 128), f32),
                vm((1, 2, 128), f32),
                dma((10,)),
                dma((12,)),
                dma((12,)),
                dma((2, STEPS)),
                dma((2, STEPS)),
                dma((2, STEPS)),
                dma((2, STEPS)),
                dma((4,)),
                dma((4,)),
                dma((3,)),
            ],
            compiler_params=pltpu.CompilerParams(collective_id=0, has_side_effects=True),
        )(
            jnp.transpose(now, (0, 2, 1, 3)),
            jnp.transpose(nxt, (0, 2, 1, 3)),
            lam,
            mu,
            jnp.transpose(dens, (1, 0, 2)),
            flags,
            slope,
            ns,
            owner,
        )
        return jnp.transpose(cur, (0, 2, 1, 3)), jnp.transpose(fol, (0, 2, 1, 3)), patch

    return jax.shard_map(
        on_device,
        mesh=mesh,
        in_specs=(
            P(None, "dom", "depth", None),
            P(None, "dom", "depth", None),
            P("dom", "depth", None),
            P("dom", "depth", None),
            P("dom", "depth", None),
            P(None, "depth", "dom", None),
            P("depth", "dom", None),
            P("depth", "dom", None),
            P("depth", "dom"),
        ),
        out_specs=(
            P(None, "dom", "depth", None),
            P(None, "dom", "depth", None),
            P("depth", "dom", None),
        ),
        check_vma=False,
    )
```

time: 54.2 us -> 43.7 us (0.81)
  Pallas kernels: 46.5 us -> 40.1 us
  local copies, waits for them, and re-layouts: 6.52 us -> 2.81 us
    pallas_call x1, Pallas kernels: 46.5 us -> 40.1 us  [on_device(): pl.pallas_call(functools.partial(kernel, nd, ndp), name='rupture', out_sh...]
    pallas_call x2 -> x0, local copies, waits for them, and re-layouts: 2.29 us -> none  [on_device(): pl.pallas_call(functools.partial(kernel, nd, ndp), name='rupture', out_sh...]
    unnamed x10 -> x7, local copies, waits for them, and re-layouts: 4.23 us -> 2.81 us
where the time goes in v1:
time: 43.7 us; the launch traced here: 43.5 us
  Pallas kernels  40.1 us (92%)
  local copies, waits for them, and re-layouts  2.81 us (6%)
  between operations  0.65 us (1%)
    pallas_call x1, Pallas kernels, on_device(): pl.pallas_call(functools.partial(kernel, nd, ndp), name='rupture', out_sh...  40.1 us
    unnamed x7, local copies, waits for them, and re-layouts  2.81 us

profile of v1, /device:TPU:32, one launch (start us, length us, event | category | flops | bytes accessed | tf_op | source)
XLA Modules:
  0.0 43.5 jit_solution(10408410399602134671)
XLA Ops:
  0.6 40.1 %rupture.1 = (f32[3,17,4,128]{3,2,1,0:T(4,128)}, f32[3,17,4,128]{3,2,1,0:T(4,128)}, f32[1,2,128]{2,1,0:T(2,128)}) custom-call(f32[3,17,4,128]{3,2,1,0:T(4,128)} %bitcast.7, f32[3,17,4,128]{3,2,1,0:T(4,128)} %bitcast.8, f32[1,4,32]{2,1,0:T(4,128)} %lam.1, f32[1,4,32]{2,1,0:T(4,128)} %mu.1, f32[17,4,128]{2,1,0:T(4,128)} %bitcast.9, s32[4,1,4,128]{3,2,1,0:T(4,128)} %flags.1, ...), custom_call_target="tpu_custom_call" | custom-call | tf_op jit(solution)/shard_map/rupture/pallas_call | solution.py:680
  40.7 0.0 copy-start
  40.7 1.6 %copy.15 = f32[3,4,17,128]{3,1,2,0:T(4,128)} copy(f32[3,4,17,128]{3,1,2,0:T(4,128)} %bitcast.6) | data formatting | bytes 208896
  42.3 0.0 copy-done
  42.3 0.0 copy-start.1
  42.3 0.6 %copy.16 = f32[3,4,17,128]{3,1,2,0:T(4,128)} copy(f32[3,4,17,128]{3,1,2,0:T(4,128)S(1)} %bitcast.5) | data formatting | bytes 208896
  42.9 0.0 copy-done.1
  43.0 0.6 %copy.17 = f32[1,2,128]{2,1,0:T(2,128)} copy(f32[1,2,128]{2,1,0:T(2,128)S(1)} %copy-done.1) | data formatting | bytes 2048
Async XLA Ops:
  40.7 1.6 %copy-start = (f32[3,17,4,128]{3,2,1,0:T(4,128)S(1)}, f32[3,17,4,128]{3,2,1,0:T(4,128)}, u32[]{:S(2)}) copy-start(f32[3,17,4,128]{3,2,1,0:T(4,128)} %get-tuple-element.7) | copy-start | bytes 313348
  42.3 0.7 %copy-start.1 = (f32[1,2,128]{2,1,0:T(2,128)S(1)}, f32[1,2,128]{2,1,0:T(2,128)}, u32[]{:S(2)}) copy-start(f32[1,2,128]{2,1,0:T(2,128)} %get-tuple-element.14) | copy-start | bytes 3076

commit v2 on v1

--- a/solution.py
+++ b/solution.py
@@ -107,8 +107,6 @@
     recv_dep,
     psend,
     precv,
-    outv,
-    patchv,
     lsem,
     isend,
     irecv,
@@ -118,7 +116,6 @@
     frecv,
     pss,
     prs,
-    osem,
 ):
     me = lax.axis_index("dom")
     my = lax.axis_index("depth")
@@ -162,6 +159,8 @@
     ]
     for cp in locals_:
         cp.start()
+    for cp in locals_[:4]:
+        cp.wait()
     pl.semaphore_wait(barrier, count)
 
     def remote(i, src, dst, to):
@@ -175,7 +174,7 @@
         )
 
     to_left = [
-        remote(0, now.at[:, :, 0:1, :], nowv.at[0, :, :, 4:5, :], (me - 1, my)),
+        remote(0, nowv.at[0, :, :, 0:1, :], nowv.at[0, :, :, 4:5, :], (me - 1, my)),
         remote(1, nxt.at[:, :, 0:1, :], nxtv.at[:, :, 4:5, :], (me - 1, my)),
         remote(2, dens.at[:, 0:1, :], densv.at[:, 4:5, :], (me - 1, my)),
         remote(3, flags, gflag.at[0], (me - 1, my)),
@@ -188,7 +187,7 @@
         remote(8, slope, gslope.at[2], (me, up)),
     ]
     to_right = [
-        remote(9, now, nowv.at[1, :, :, 0:4, :], (me + 1, my)),
+        remote(9, nowv.at[0, :, :, 0:4, :], nowv.at[1, :, :, 0:4, :], (me + 1, my)),
         remote(10, lam, modv.at[1, 0], (me + 1, my)),
         remote(11, mu, modv.at[1, 1], (me + 1, my)),
     ]
@@ -387,14 +386,10 @@
             def _(i=i):
                 patch_copy(i).start()
 
-        patchv[0, pl.ds(0, 1), :] = members(0, 0)
-        patchv[0, pl.ds(1, 1), :] = members(0, 1)
-
-    out_copies = [
-        pltpu.make_async_copy(outv.at[0, :, :, 0:4, :], out_cur, osem.at[0]),
-        pltpu.make_async_copy(outv.at[1, :, :, 0:4, :], out_fol, osem.at[1]),
-        pltpu.make_async_copy(patchv, out_patch, osem.at[2]),
-    ]
+        out_patch[0, pl.ds(0, 1), :] = members(0, 0)
+        out_patch[0, pl.ds(1, 1), :] = members(0, 1)
+
+    outs = (out_cur, out_fol)
 
     def from_elements(slot, which):
         for c in range(3):
@@ -405,8 +400,7 @@
             for y in range(17):
                 ey, yl = (y // 4, y % 4) if y < 16 else (3, 4)
                 v = pick(*[roll(e(yl, zl), 32 * (zl - ey)) for zl in range(4)])
-                outv[which, c, y] = permute(v, to_natural)
-        out_copies[which].start()
+                outs[which][c, y] = permute(v, to_natural)[0:4]
 
     grad[...] = jnp.zeros((8, 128), f32)
 
@@ -427,8 +421,6 @@
         def _():
             @pl.when(is_left)
             def _():
-                locals_[1].wait()
-
                 @pl.when(has_l)
                 def _():
                     for cp in to_right:
@@ -438,8 +430,6 @@
 
             @pl.when(own)
             def _():
-                for cp in (locals_[0], locals_[2], locals_[3]):
-                    cp.wait()
                 put_moduli(0)
 
                 @pl.when(has_r)
@@ -636,9 +626,7 @@
         @pl.when(inside(me - off))
         def _(i=i):
             patch_copy(i).wait_recv()
-            patchv[0] = patchv[0] + precv[i, pl.ds(0, 2), :]
-
-    out_copies[2].start()
+            out_patch[0] = out_patch[0] + precv[i, pl.ds(0, 2), :]
 
     @pl.when(has_l)
     def _():
@@ -665,7 +653,13 @@
         def _(i=i):
             patch_copy(i).wait_send()
 
-    for cp in out_copies:
+
+def store_results(cur, fol, patch, out_cur, out_fol, out_patch, sem):
+    pairs = ((cur, out_cur), (fol, out_fol), (patch, out_patch))
+    copies = [pltpu.make_async_copy(a, b, sem.at[i]) for i, (a, b) in enumerate(pairs)]
+    for cp in copies:
+        cp.start()
+    for cp in copies:
         cp.wait()
 
 
@@ -681,12 +675,12 @@
             functools.partial(kernel, nd, ndp),
             name="rupture",
             out_shape=(
-                jax.ShapeDtypeStruct((3, 17, 4, 128), f32),
-                jax.ShapeDtypeStruct((3, 17, 4, 128), f32),
-                jax.ShapeDtypeStruct((1, 2, 128), f32),
+                vm((3, 17, 4, 128), f32),
+                vm((3, 17, 4, 128), f32),
+                vm((1, 2, 128), f32),
             ),
             in_specs=[any_] * 9,
-            out_specs=[any_] * 3,
+            out_specs=[pl.BlockSpec(memory_space=pltpu.VMEM)] * 3,
             scratch_shapes=[
                 vm((2, 3, 17, 8, 128), f32),
                 vm((3, 17, 8, 128), f32),
@@ -714,8 +708,6 @@
                 vm((2, STEPS, 3, 8, 128), f32),
                 vm((4, 8, 128), f32),
                 vm((4, 8, 128), f32),
-                vm((2, 3, 17, 8, 128), f32),
-                vm((1, 2, 128), f32),
                 dma((10,)),
                 dma((12,)),
                 dma((12,)),
@@ -725,7 +717,6 @@
                 dma((2, STEPS)),
                 dma((4,)),
                 dma((4,)),
-                dma((3,)),
             ],
             compiler_params=pltpu.CompilerParams(collective_id=0, has_side_effects=True),
         )(
@@ -739,6 +730,18 @@
             ns,
             owner,
         )
+        cur, fol, patch = pl.pallas_call(
+            store_results,
+            name="store_results",
+            out_shape=(
+                jax.ShapeDtypeStruct((3, 17, 4, 128), f32),
+                jax.ShapeDtypeStruct((3, 17, 4, 128), f32),
+                jax.ShapeDtypeStruct((1, 2, 128), f32),
+            ),
+            in_specs=[pl.BlockSpec(memory_space=pltpu.VMEM)] * 3,
+            out_specs=[any_] * 3,
+            scratch_shapes=[dma((3,))],
+        )(*[pltpu.with_memory_space_constraint(v, pltpu.VMEM) for v in (cur, fol, patch)])
         return jnp.transpose(cur, (0, 2, 1, 3)), jnp.transpose(fol, (0, 2, 1, 3)), patch
 
     return jax.shard_map(

time: 43.7 us -> 40.8 us (0.934)
  local copies, waits for them, and re-layouts: 2.81 us -> 0 us
    unnamed x7 -> x0, local copies, waits for them, and re-layouts: 2.81 us -> none
    pallas_call x1, Pallas kernels: 40.1 us -> 39.3 us  [on_device(): pl.pallas_call(functools.partial(kernel, nd, ndp), name='rupture', out_sh...]
    pallas_call x0 -> x1, Pallas kernels: none -> 0.71 us  [on_device(): pl.pallas_call(store_results, name='store_results', out_shape=(jax.ShapeD...]
where the time goes in v2:
time: 40.8 us; the launch traced here: 40.7 us
  Pallas kernels  40 us (98%)
  between operations  0.64 us (2%)
    pallas_call x1, Pallas kernels, on_device(): pl.pallas_call(functools.partial(kernel, nd, ndp), name='rupture', out_sh...  39.3 us

profile of v2, /device:TPU:32, one launch (start us, length us, event | category | flops | bytes accessed | tf_op | source)
XLA Modules:
  0.0 40.7 jit_solution(17997319762684054457)
XLA Ops:
  0.6 39.3 %rupture.1 = (f32[3,17,4,128]{3,2,1,0:T(4,128)S(1)}, f32[3,17,4,128]{3,2,1,0:T(4,128)S(1)}, f32[1,2,128]{2,1,0:T(2,128)S(1)}) custom-call(f32[3,17,4,128]{3,2,1,0:T(4,128)} %bitcast.5, f32[3,17,4,128]{3,2,1,0:T(4,128)} %bitcast.6, f32[1,4,32]{2,1,0:T(4,128)} %lam.1, f32[1,4,32]{2,1,0:T(4,128)} %mu.1, f32[17,4,128]{2,1,0:T(4,128)} %bitcast.7, ...), custom_call_target="tpu_custom_call" | custom-call | tf_op jit(solution)/shard_map/rupture/pallas_call | solution.py:674
  40.0 0.7 %store_results.1 = (f32[3,17,4,128]{3,2,1,0:T(4,128)}, f32[3,17,4,128]{3,2,1,0:T(4,128)}, f32[1,2,128]{2,1,0:T(2,128)}) custom-call(f32[3,17,4,128]{3,2,1,0:T(4,128)S(1)} %get-tuple-element.9.cur, f32[3,17,4,128]{3,2,1,0:T(4,128)S(1)} %get-tuple-element.10.fol, f32[1,2,128]{2,1,0:T(2,128)S(1)} %get-tuple-element.11.patch), custom_call_target="tpu_custom_call" | custom-call | tf_op jit(solution)/shard_map/store_results/pallas_call | solution.py:733

commit v3 on v2

--- a/solution.py
+++ b/solution.py
@@ -91,6 +91,11 @@
     ownv,
     gflag,
     gslope,
+    gnow,
+    gnxt,
+    gdens,
+    GS,
+    DE,
     S,
     F,
     GY,
@@ -116,6 +121,7 @@
     frecv,
     pss,
     prs,
+    far,
 ):
     me = lax.axis_index("dom")
     my = lax.axis_index("depth")
@@ -127,7 +133,7 @@
 
     barrier = pltpu.get_barrier_semaphore()
     count = 2
-    for off, row in ((-1, my), (1, my), (-2, my), (2, my), (-1, up), (1, dn)):
+    for off, row in ((1, my), (-1, my), (-1, up), (1, dn)):
         ok = jnp.logical_and(me + off >= 0, me + off < nd)
         count = count + ok.astype(jnp.int32)
 
@@ -159,7 +165,7 @@
     ]
     for cp in locals_:
         cp.start()
-    for cp in locals_[:4]:
+    for cp in locals_[:6]:
         cp.wait()
     pl.semaphore_wait(barrier, count)
 
@@ -174,9 +180,9 @@
         )
 
     to_left = [
-        remote(0, nowv.at[0, :, :, 0:1, :], nowv.at[0, :, :, 4:5, :], (me - 1, my)),
-        remote(1, nxt.at[:, :, 0:1, :], nxtv.at[:, :, 4:5, :], (me - 1, my)),
-        remote(2, dens.at[:, 0:1, :], densv.at[:, 4:5, :], (me - 1, my)),
+        remote(0, nowv.at[0, :, :, 0, :], gnow.at[:, 0:17, :], (me - 1, my)),
+        remote(1, nxtv.at[:, :, 0, :], gnxt.at[:, 0:17, :], (me - 1, my)),
+        remote(2, densv.at[:, 0, :], gdens.at[0, 0:17, :], (me - 1, my)),
         remote(3, flags, gflag.at[0], (me - 1, my)),
         remote(4, slope, gslope.at[0], (me - 1, my)),
         remote(5, flags, gflag.at[1], (me - 1, up)),
@@ -208,6 +214,11 @@
 
     for cp in to_up:
         cp.start()
+
+    @pl.when(jnp.logical_and(has_l, has_r))
+    def _():
+        pl.semaphore_signal(far.at[0], inc=1, device_id=(me - 1, my), device_id_type=MESH)
+        pl.semaphore_signal(far.at[1], inc=1, device_id=(me + 1, my), device_id_type=MESH)
 
     lane = lax.broadcasted_iota(jnp.int32, (8, 128), 1)
     sub = lax.broadcasted_iota(jnp.int32, (8, 128), 0)
@@ -293,22 +304,58 @@
                 live, (8.0 * DT2) / jnp.where(live, mass, 1.0), 0.0
             )
 
-        to_elements(lambda y: jnp.where(live_x, densv[y], 1.0), put_mass, 1.0)
-        for c in range(3):
-            for i in range(25):
-                IMP[0, pl.ds(25 * c + i, 1), :] = IM[pl.ds(8 * i, 1), :]
-                IMP[1, pl.ds(25 * c + i, 1), :] = IM[pl.ds(8 * i + 4, 1), :]
-        for i in range(75, ROWS):
-            IMP[0, pl.ds(i, 1), :] = jnp.zeros((1, 128), f32)
-            IMP[1, pl.ds(i, 1), :] = jnp.zeros((1, 128), f32)
-
-    def following_field():
-        for c in range(3):
-
-            def put(yl, zl, v, c=c):
-                S[1, pl.ds(8 * rblk(c, yl, zl), 8), :] = v
-
-            to_elements(lambda y, c=c: jnp.where(live_x, nxtv[c, y], 0.0), put, 0.0)
+        for yl in range(5):
+            for zl in range(5):
+                put_mass(yl, zl, DE[pl.ds(8 * (yl * 5 + zl), 8), :])
+        for plane, x in ((0, 0), (1, 4)):
+            for g in range(4):
+                n = 8 if g < 3 else 1
+                v = IM[pl.ds(64 * g + x, n, stride=8), :] if n > 1 else IM[pl.ds(64 * g + x, 1), :]
+                for c in range(3):
+                    IMP[plane, pl.ds(25 * c + 8 * g, n), :] = v
+            IMP[plane, pl.ds(75, 5), :] = jnp.zeros((5, 128), f32)
+
+    def own_rows(load, outside, put):
+        to_elements(lambda y: jnp.where(sub < 4, load(y), outside), put, outside)
+
+    def own_fields():
+        for slot in range(2):
+            for c in range(3):
+
+                def put(yl, zl, v, slot=slot, c=c):
+                    S[slot, pl.ds(8 * rblk(c, yl, zl), 8), :] = v
+
+                if slot == 0:
+                    own_rows(lambda y, c=c: nowv[0, c, y], 0.0, put)
+                else:
+                    own_rows(lambda y, c=c: nxtv[c, y], 0.0, put)
+
+        def put_dens(yl, zl, v):
+            DE[pl.ds(8 * (yl * 5 + zl), 8), :] = v
+
+        own_rows(lambda y: densv[y], 1.0, put_dens)
+
+    def ghost_plane(ref, comps, bottom, put):
+        for c in range(comps):
+            for g in range(3):
+                v = permute(ref[c, pl.ds(8 * g, 8), :], to_packed)
+                for k in range(4):
+                    GS[c, k, pl.ds(8 * g, 8), :] = roll(v, 32 * k)
+        for c in range(comps):
+            for zl in range(4):
+                v = pick(*[GS[c, (e - zl) % 4, pl.ds(4 * e, 8), :] for e in range(4)])
+                put(c, zl, v[0:5])
+                if zl == 0:
+                    put(c, 4, jnp.where(ez == 31, bottom, roll(v, -1))[0:5])
+
+    def put_ghost(slot):
+        def put(c, zl, v):
+            S[slot, pl.ds(8 * rblk(c, 0, zl) + 4, 5, stride=40), :] = v
+
+        return put
+
+    def put_ghost_dens(c, zl, v):
+        DE[pl.ds(8 * zl + 4, 5, stride=40), :] = v
 
     def fault_tables():
         def planes(own, ghost):
@@ -403,6 +450,8 @@
                 outs[which][c, y] = permute(v, to_natural)[0:4]
 
     grad[...] = jnp.zeros((8, 128), f32)
+    put_moduli(0)
+    own_fields()
 
     def turn(it, carry):
         step = jnp.maximum(it - 1, 0)
@@ -417,36 +466,25 @@
         src = cur + 2 * fs
         cb = 10 + 12 * fs
 
-        @pl.when(it < 2)
+        @pl.when(is_left)
         def _():
-            @pl.when(is_left)
+            @pl.when(has_l)
             def _():
-                @pl.when(has_l)
-                def _():
-                    for cp in to_right:
-                        cp.wait_recv()
-
-                put_moduli(1)
-
-            @pl.when(own)
-            def _():
-                put_moduli(0)
-
-                @pl.when(has_r)
-                def _():
-                    to_left[0].wait_recv()
-
-            live = jnp.logical_or(
-                sub < 4, jnp.logical_and(sub == 4, jnp.logical_or(is_left, has_r))
-            )
+                for cp in to_right:
+                    cp.wait_recv()
+
+            put_moduli(1)
             for c in range(3):
 
                 def put(yl, zl, v, c=c):
-                    S[src, pl.ds(8 * rblk(c, yl, zl), 8), :] = v
-
-                to_elements(
-                    lambda y, c=c: jnp.where(live, nowv[fs, c, y], 0.0), put, 0.0
-                )
+                    S[2, pl.ds(8 * rblk(c, yl, zl), 8), :] = v
+
+                to_elements(lambda y, c=c: jnp.where(sub < 5, nowv[1, c, y], 0.0), put, 0.0)
+
+        @pl.when(jnp.logical_and(jnp.logical_and(own, it < 2), has_r))
+        def _():
+            to_left[0].wait_recv()
+            ghost_plane(gnow, 3, 0.0, put_ghost(0))
 
         def u(c, yl, zl):
             return S[src, pl.ds(8 * rblk(c, yl, zl), 8), :]
@@ -545,9 +583,9 @@
             def _():
                 dom_copy(1, step).start()
 
-        @pl.when(it == 1)
+        @pl.when(it == odd.astype(jnp.int32))
         def _():
-            for cp in locals_[4:]:
+            for cp in locals_[6:]:
                 cp.wait()
             for cp in to_up:
                 cp.wait_recv()
@@ -556,8 +594,9 @@
             def _():
                 for cp in to_left[1:]:
                     cp.wait_recv()
-
-            following_field()
+                ghost_plane(gnxt, 3, 0.0, put_ghost(1))
+                ghost_plane(gdens, 1, 1.0, put_ghost_dens)
+
             mass_table()
             fault_tables()
 
@@ -572,36 +611,55 @@
                     grad[...] = grad[...] + TH[2, step] * slip_hi
                 hi = (LOCK if c == 1 else TH[0, step]) * slip_hi
                 lo = (LOCK if c == 1 else TH[1, step]) * slip_lo
+                rh = [pl.ds(8 * rblk(c, 4, zl), 8) for zl in range(5)]
+                rl = [pl.ds(8 * rblk(c, 0, zl), 8) for zl in range(5)]
+                vh, vl = [], []
                 for zl in range(5):
                     sh = (96, 0) if zl < 4 else (95, -1)
                     zb = zl if zl < 4 else 0
-                    rh, rl = pl.ds(8 * rblk(c, 4, zl), 8), pl.ds(8 * rblk(c, 0, zl), 8)
-                    F[0, rh, :] = F[0, rh, :] - jnp.where(
-                        b3, roll(hi, sh[0] - 32 * zb), 0.0
+                    vh.append(
+                        F[0, rh[zl], :] - jnp.where(b3, roll(hi, sh[0] - 32 * zb), 0.0)
                     )
-                    F[0, rl, :] = F[0, rl, :] + jnp.where(
-                        b0, roll(lo, sh[1] - 32 * zb), 0.0
+                    vl.append(
+                        F[0, rl[zl], :] + jnp.where(b0, roll(lo, sh[1] - 32 * zb), 0.0)
                     )
+                for zl in range(5):
+                    F[0, rh[zl], :] = vh[zl]
+                    F[0, rl[zl], :] = vl[zl]
 
             for yl in range(5):
-                for zl in range(5):
-                    im = IM[pl.ds(8 * (yl * 5 + zl), 8), :]
-                    for c in range(3):
-                        r = pl.ds(8 * rblk(c, yl, zl), 8)
-                        now_u = S[cur, r, :]
-                        S[new, r, :] = (now_u + now_u) - S[new, r, :] - im * F[0, r, :]
+                rs = [pl.ds(8 * rblk(c, yl, zl), 8) for zl in range(5) for c in range(3)]
+                ims = [IM[pl.ds(8 * (yl * 5 + zl), 8), :] for zl in range(5)]
+                news = []
+                for i, r in enumerate(rs):
+                    now_u = S[cur, r, :]
+                    news.append((now_u + now_u) - S[new, r, :] - ims[i // 3] * F[0, r, :])
+                for r, v in zip(rs, news):
+                    S[new, r, :] = v
 
             @pl.when(it == STEPS)
             def _():
+                @pl.when(me + 2 < nd)
+                def _():
+                    pl.semaphore_wait(far.at[0], 1)
+
+                @pl.when(me - 2 >= 0)
+                def _():
+                    pl.semaphore_wait(far.at[1], 1)
+
                 send_patches()
                 from_elements(1 - STEPS % 2, 1)
 
             def add_side(side, first):
                 plane = 0 if first == 0 else 1
-                for g in range(ROWS // 8):
-                    r = pl.ds(64 * g + first, 8, stride=8)
-                    d = pl.ds(8 * g, 8)
-                    S[new, r, :] = S[new, r, :] - IMP[plane, d, :] * recv_dom[side, step, d, :]
+                rs = [pl.ds(64 * g + first, 8, stride=8) for g in range(ROWS // 8)]
+                ds = [pl.ds(8 * g, 8) for g in range(ROWS // 8)]
+                news = [
+                    S[new, r, :] - IMP[plane, d, :] * recv_dom[side, step, d, :]
+                    for r, d in zip(rs, ds)
+                ]
+                for r, v in zip(rs, news):
+                    S[new, r, :] = v
 
             @pl.when(has_r)
             def _():
@@ -692,6 +750,11 @@
                 pltpu.SMEM((1, 4), i32),
                 vm((3, 4, 1, 4, 128), i32),
                 vm((3, 1, 4, 128), f32),
+                vm((3, 24, 128), f32),
+                vm((3, 24, 128), f32),
+                vm((1, 24, 128), f32),
+                vm((3, 4, 24, 128), f32),
+                vm((25 * 8, 128), f32),
                 vm((3, ROWS * 8, 128), f32),
                 vm((2, ROWS * 8, 128), f32),
                 vm((ROWS * 8, 128), f32),
@@ -717,6 +780,7 @@
                 dma((2, STEPS)),
                 dma((4,)),
                 dma((4,)),
+                pltpu.SemaphoreType.REGULAR((2,)),
             ],
             compiler_params=pltpu.CompilerParams(collective_id=0, has_side_effects=True),
         )(

time: 40.8 us -> 40 us (0.980)
  Pallas kernels: 40 us -> 39.2 us
    pallas_call x1, Pallas kernels: 39.3 us -> 38.5 us  [on_device(): pl.pallas_call(functools.partial(kernel, nd, ndp), name='rupture', out_sh...]
where the time goes in v3:
time: 40 us; the launch traced here: 39.8 us
  Pallas kernels  39.2 us (98%)
  between operations  0.64 us (2%)
    pallas_call x1, Pallas kernels, on_device(): pl.pallas_call(functools.partial(kernel, nd, ndp), name='rupture', out_sh...  38.5 us

profile of v3, /device:TPU:32, one launch (start us, length us, event | category | flops | bytes accessed | tf_op | source)
XLA Modules:
  0.0 39.8 jit_solution(11212692480411358236)
XLA Ops:
  0.6 38.5 %rupture.1 = (f32[3,17,4,128]{3,2,1,0:T(4,128)S(1)}, f32[3,17,4,128]{3,2,1,0:T(4,128)S(1)}, f32[1,2,128]{2,1,0:T(2,128)S(1)}) custom-call(f32[3,17,4,128]{3,2,1,0:T(4,128)} %bitcast.5, f32[3,17,4,128]{3,2,1,0:T(4,128)} %bitcast.6, f32[1,4,32]{2,1,0:T(4,128)} %lam.1, f32[1,4,32]{2,1,0:T(4,128)} %mu.1, f32[17,4,128]{2,1,0:T(4,128)} %bitcast.7, ...), custom_call_target="tpu_custom_call" | custom-call | tf_op jit(solution)/shard_map/rupture/pallas_call | solution.py:732
  39.1 0.7 %store_results.1 = (f32[3,17,4,128]{3,2,1,0:T(4,128)}, f32[3,17,4,128]{3,2,1,0:T(4,128)}, f32[1,2,128]{2,1,0:T(2,128)}) custom-call(f32[3,17,4,128]{3,2,1,0:T(4,128)S(1)} %get-tuple-element.9.cur, f32[3,17,4,128]{3,2,1,0:T(4,128)S(1)} %get-tuple-element.10.fol, f32[1,2,128]{2,1,0:T(2,128)S(1)} %get-tuple-element.11.patch), custom_call_target="tpu_custom_call" | custom-call | tf_op jit(solution)/shard_map/store_results/pallas_call | solution.py:797

commit v4 on v3

--- a/solution.py
+++ b/solution.py
@@ -575,7 +575,7 @@
                 send_dom[0, step, d, :] = F[0, pl.ds(64 * g, 8, stride=8), :]
                 send_dom[1, step, d, :] = F[0, pl.ds(64 * g + 4, 8, stride=8), :]
 
-            @pl.when(has_l)
+            @pl.when(jnp.logical_and(has_l, step < STEPS - 1))
             def _():
                 dom_copy(0, step).start()
 
@@ -661,18 +661,25 @@
                 for r, v in zip(rs, news):
                     S[new, r, :] = v
 
-            @pl.when(has_r)
+            def left_side():
+                @pl.when(step > 0)
+                def _():
+                    dom_copy(1, step).wait_recv()
+
+                add_side(1, 0)
+
+            @pl.when(jnp.logical_and(has_l, odd))
+            def _():
+                left_side()
+
+            @pl.when(jnp.logical_and(has_r, step < STEPS - 1))
             def _():
                 dom_copy(0, step).wait_recv()
                 add_side(0, 4)
 
-            @pl.when(has_l)
+            @pl.when(jnp.logical_and(has_l, jnp.logical_not(odd)))
             def _():
-                @pl.when(step > 0)
-                def _():
-                    dom_copy(1, step).wait_recv()
-
-                add_side(1, 0)
+                left_side()
 
         return carry
 
@@ -690,7 +697,7 @@
     def _():
         for cp in to_left:
             cp.wait_send()
-        for s in range(STEPS):
+        for s in range(STEPS - 1):
             dom_copy(0, s).wait_send()
 
     @pl.when(has_r)

time: 40 us -> 40 us (level)
  no operation moved by 1% of the time
where the time goes in v4:
time: 40 us; the launch traced here: 39.8 us
  Pallas kernels  39.2 us (98%)
  between operations  0.64 us (2%)
    pallas_call x1, Pallas kernels, on_device(): pl.pallas_call(functools.partial(kernel, nd, ndp), name='rupture', out_sh...  38.5 us

profile of v4, /device:TPU:32, one launch (start us, length us, event | category | flops | bytes accessed | tf_op | source)
XLA Modules:
  0.0 39.8 jit_solution(6568218861001566866)
XLA Ops:
  0.6 38.5 %rupture.1 = (f32[3,17,4,128]{3,2,1,0:T(4,128)S(1)}, f32[3,17,4,128]{3,2,1,0:T(4,128)S(1)}, f32[1,2,128]{2,1,0:T(2,128)S(1)}) custom-call(f32[3,17,4,128]{3,2,1,0:T(4,128)} %bitcast.5, f32[3,17,4,128]{3,2,1,0:T(4,128)} %bitcast.6, f32[1,4,32]{2,1,0:T(4,128)} %lam.1, f32[1,4,32]{2,1,0:T(4,128)} %mu.1, f32[17,4,128]{2,1,0:T(4,128)} %bitcast.7, ...), custom_call_target="tpu_custom_call" | custom-call | tf_op jit(solution)/shard_map/rupture/pallas_call | solution.py:739
  39.1 0.7 %store_results.1 = (f32[3,17,4,128]{3,2,1,0:T(4,128)}, f32[3,17,4,128]{3,2,1,0:T(4,128)}, f32[1,2,128]{2,1,0:T(2,128)}) custom-call(f32[3,17,4,128]{3,2,1,0:T(4,128)S(1)} %get-tuple-element.9.cur, f32[3,17,4,128]{3,2,1,0:T(4,128)S(1)} %get-tuple-element.10.fol, f32[1,2,128]{2,1,0:T(2,128)S(1)} %get-tuple-element.11.patch), custom_call_target="tpu_custom_call" | custom-call | tf_op jit(solution)/shard_map/store_results/pallas_call | solution.py:804
